TPU v7x, 256 devices: a whole 4x4x8 slice. The times are simulated.
256 devices in a mesh: dp: 8 (over x, y_hi), row: 4 (over y_lo, core), col: 8 (over z).
Axes of the slice: x: 4, y: 4 (y_hi: 2, y_lo: 2; y = y_hi * 2 + y_lo), z: 8, core: 2. Of those that a mesh axis runs over, the one named last changes fastest.
Arguments:
- teacher_in: bfloat16 [8, 128, 256, 384], P('dp', 'row', 'col'), may hold values from -6 to 6
- student_in: bfloat16 [8, 128, 256, 384], P('dp', 'row', 'col'), may hold values from -6 to 6
- cotangent: bfloat16 [8, 128, 256, 384], P('dp', 'row', 'col'), may hold values from -6 to 6
- kernels: bfloat16 [2, 49, 384], replicated, may hold values from -0.875 to 0.875
- norm_gains: bfloat16 [2, 2, 384], replicated, may hold values from 0.25 to 1.75
- biases: bfloat16 [2, 3, 384], replicated, may hold values from -3 to 3
- weight_in: bfloat16 [2, 384, 1536], P(None, None, 'dp'), may hold values from -0.3125 to 0.3125
- bias_in: bfloat16 [2, 1536], P(None, 'dp'), may hold values from -3 to 3
- weight_out: bfloat16 [2, 1536, 384], P(None, 'dp'), may hold values from -0.15625 to 0.15625
Outputs:
- teacher_out: float32 [8, 128, 256, 384], P('dp', 'row', 'col')
- student_out: float32 [8, 128, 256, 384], P('dp', 'row', 'col')
- input_grad: float32 [8, 128, 256, 384], P('dp', 'row', 'col')
- grad_weight_in: float32 [384, 1536], P(None, 'dp')
- grad_bias_in: float32 [1536], P('dp')
- grad_weight_out: float32 [1536, 384], P('dp')
- grad_kernel: float32 [49, 384], replicated
- grad_gains: float32 [2, 384], replicated
- grad_biases: float32 [3, 384], replicated
All inputs are finite; a program needn't handle non-finite values.
Results may differ from a plain program's by a relative error of at most 0.0057.
Values may be sent and summed in bfloat16 or wider, within the bound.
No kernel may reach another device: no remote copies, remote signals or barrier semaphores. Data moves between devices by JAX's collectives and lax.ppermute only.
A program may use at most 128 MiB of HBM per device.

v0:
```python
import jax
import jax.numpy as jnp
from jax import lax
from jax.sharding import PartitionSpec as P

KERNEL = 7
EPSILON = 1e-06
ROOT_HALF = 0.7071067811865476
INV_ROOT_TWO_PI = 0.3989422804014327


def with_halo(value, sides, width):
    for axis, dim in sides:
        peers, length = (lax.axis_size(axis), value.shape[dim])
        up = [(i, (i + 1) % peers) for i in range(peers - 1)]
        down = [(j, i) for i, j in up]
        last = lax.slice_in_dim(value, length - width, length, axis=dim)
        leading = lax.slice_in_dim(value, 0, width, axis=dim)
        before = lax.ppermute(last, axis, up)
        after = lax.ppermute(leading, axis, down)
        value = jnp.concatenate([before, value, after], axis=dim)
    return value


def gelu_value(before):
    return before * 0.5 * (1.0 + lax.erf(before * ROOT_HALF))


def gelu_slope(before):
    return 0.5 * (1.0 + lax.erf(before * ROOT_HALF)) + before * INV_ROOT_TWO_PI * jnp.exp(
        -0.5 * before * before
    )


def depthwise(padded, kernel, height, breadth):
    running = jnp.zeros((padded.shape[0], height, breadth, padded.shape[3]), jnp.float32)
    for position in range(KERNEL * KERNEL):
        vertical = position // KERNEL
        lateral = position % KERNEL
        window = padded[:, vertical : vertical + height, lateral : lateral + breadth, :]
        running = running + window.astype(jnp.float32) * kernel[position].astype(jnp.float32)
    return running


def forward(padded, inputs, kernel, norm_gains, biases, weight_in, bias_in, weight_out):
    height, breadth, channels = (inputs.shape[1], inputs.shape[2], inputs.shape[3])
    convolved = depthwise(padded, kernel, height, breadth) + biases[0].astype(jnp.float32)
    centered = convolved - jnp.mean(convolved, axis=-1, keepdims=True)
    inverse = lax.rsqrt(jnp.mean(centered * centered, axis=-1, keepdims=True) + EPSILON)
    scaled = centered * inverse
    normed = (scaled * norm_gains[0].astype(jnp.float32) + biases[1].astype(jnp.float32)).astype(
        jnp.bfloat16
    )
    normed = normed.reshape(-1, channels)
    before = jnp.dot(normed, weight_in, preferred_element_type=jnp.float32) + bias_in.astype(
        jnp.float32
    )
    hidden = gelu_value(before).astype(jnp.bfloat16)
    branch = jnp.dot(hidden, weight_out, preferred_element_type=jnp.float32) + biases[2].astype(
        jnp.float32
    )
    output = inputs.astype(jnp.float32) + norm_gains[1].astype(jnp.float32) * branch.reshape(
        inputs.shape
    )
    return (output, (scaled, inverse, normed, before, hidden, branch))


def backward(cotangent, padded, stored, norm_gains, weight_in, weight_out):
    scaled, inverse, normed, before, hidden, branch = stored
    height, breadth, channels = (cotangent.shape[1], cotangent.shape[2], cotangent.shape[3])
    flat_grad = cotangent.astype(jnp.float32).reshape(-1, channels)
    grad_gamma = jnp.sum(flat_grad * branch, axis=0)
    branch_grad = (flat_grad * norm_gains[1].astype(jnp.float32)).astype(jnp.bfloat16)
    branch_grad = lax.optimization_barrier(branch_grad)
    grad_out_bias = jnp.sum(branch_grad.astype(jnp.float32), axis=0)
    grad_weight_out = jnp.dot(hidden.T, branch_grad, preferred_element_type=jnp.float32)
    hidden_grad = jnp.dot(branch_grad, weight_out.T, preferred_element_type=jnp.float32)
    before_grad = (hidden_grad * gelu_slope(before)).astype(jnp.bfloat16)
    before_grad = lax.optimization_barrier(before_grad)
    grad_bias_in = jnp.sum(before_grad.astype(jnp.float32), axis=0)
    grad_weight_in = jnp.dot(normed.T, before_grad, preferred_element_type=jnp.float32)
    normed_grad = jnp.dot(before_grad, weight_in.T, preferred_element_type=jnp.float32).reshape(
        scaled.shape
    )
    grad_norm_gain = jnp.sum(normed_grad * scaled, axis=(0, 1, 2))
    grad_norm_bias = jnp.sum(normed_grad, axis=(0, 1, 2))
    scaled_grad = normed_grad * norm_gains[0].astype(jnp.float32)
    conv_grad = inverse * (
        scaled_grad
        - jnp.mean(scaled_grad, axis=-1, keepdims=True)
        - scaled * jnp.mean(scaled_grad * scaled, axis=-1, keepdims=True)
    )
    conv_grad = lax.optimization_barrier(conv_grad.astype(jnp.bfloat16))
    conv_wide = conv_grad.astype(jnp.float32)
    grad_conv_bias = jnp.sum(conv_wide, axis=(0, 1, 2))
    tap_sums = []
    for position in range(KERNEL * KERNEL):
        vertical = position // KERNEL
        lateral = position % KERNEL
        window = padded[:, vertical : vertical + height, lateral : lateral + breadth, :].astype(
            jnp.float32
        )
        tap_sums.append(jnp.sum(window * conv_wide, axis=(0, 1, 2)))
    grad_kernel = jnp.stack(tap_sums)
    large_grads = (grad_weight_in, grad_bias_in, grad_weight_out)
    minor_grads = (
        grad_kernel,
        jnp.stack([grad_norm_gain, grad_gamma]),
        jnp.stack([grad_conv_bias, grad_norm_bias, grad_out_bias]),
    )
    return (conv_grad, large_grads, minor_grads)


def input_gradient(cotangent, padded_grad, kernel):
    height, breadth = (cotangent.shape[1], cotangent.shape[2])
    flipped = depthwise(padded_grad, kernel[::-1], height, breadth)
    return cotangent.astype(jnp.float32) + flipped


def on_device(
    teacher_in, student_in, cotangent, kernels, norm_gains, biases, weight_in, bias_in, weight_out
):
    margin = KERNEL // 2
    full_in, full_bias, full_out = (
        lax.all_gather(weight_in, "dp", axis=2, tiled=True),
        lax.all_gather(bias_in, "dp", axis=1, tiled=True),
        lax.all_gather(weight_out, "dp", axis=1, tiled=True),
    )
    teacher_pad = with_halo(teacher_in, (("row", 1), ("col", 2)), margin)
    student_pad = with_halo(student_in, (("row", 1), ("col", 2)), margin)
    teacher_res, unused = forward(
        teacher_pad,
        teacher_in,
        kernels[0],
        norm_gains[0],
        biases[0],
        full_in[0],
        full_bias[0],
        full_out[0],
    )
    student_res, stored = forward(
        student_pad,
        student_in,
        kernels[1],
        norm_gains[1],
        biases[1],
        full_in[1],
        full_bias[1],
        full_out[1],
    )
    conv_grad, large_grads, minor_grads = backward(
        cotangent, student_pad, stored, norm_gains[1], full_in[1], full_out[1]
    )
    grad_pad = with_halo(conv_grad, (("row", 1), ("col", 2)), margin)
    in_grad = input_gradient(cotangent, grad_pad, kernels[1])
    minor_sums = lax.psum((minor_grads[0], minor_grads[1], minor_grads[2]), ("dp", "row", "col"))
    owned = (
        lax.psum_scatter(large_grads[0], "dp", scatter_dimension=1, tiled=True),
        lax.psum_scatter(large_grads[1], "dp", scatter_dimension=0, tiled=True),
        lax.psum_scatter(large_grads[2], "dp", scatter_dimension=0, tiled=True),
    )
    shares = lax.psum((owned[0], owned[1], owned[2]), ("row", "col"))
    tokens = (
        teacher_in.shape[0]
        * teacher_in.shape[1]
        * teacher_in.shape[2]
        * lax.axis_size("dp")
        * lax.axis_size("row")
        * lax.axis_size("col")
    )
    factor = float(tokens) ** (-0.5)
    return (
        teacher_res,
        student_res,
        in_grad,
        shares[0] * factor,
        shares[1] * factor,
        shares[2] * factor,
        minor_sums[0] * factor,
        minor_sums[1] * factor,
        minor_sums[2] * factor,
    )


def solution(mesh):
    placed = (
        P("dp", "row", "col", None),
        P("dp", "row", "col", None),
        P("dp", "row", "col", None),
        P(),
        P(),
        P(),
        P(None, None, "dp"),
        P(None, "dp"),
        P(None, "dp", None),
    )
    return jax.shard_map(
        on_device,
        mesh=mesh,
        in_specs=placed,
        out_specs=(
            P("dp", "row", "col", None),
            P("dp", "row", "col", None),
            P("dp", "row", "col", None),
            P(None, "dp"),
            P("dp"),
            P("dp", None),
            P(),
            P(),
            P(),
        ),
        check_vma=False,
    )
```

profile of v0, /device:TPU:1, one launch (start us, length us, event | category | flops | bytes accessed | tf_op | source)
XLA Modules:
  0.0 829.3 jit_solution(6039890744320597389)
XLA Ops:
  8.9 4.6 collective-permute-start
  16.4 3.6 collective-permute-start.4
  30.5 19.7 %all-gather = bf16[8,192,2]{1,2,0:T(2,128)(2,1)S(1)} all-gather(bf16[1,192,2]{1,2,0:T(2,128)(2,1)} %bitcast.59), channel_id=1, replica_groups=mesh['dp'=8,'row'=4,'col'=8] {'dp'}, dimensions={0}, use_global_device_ids=true | all-gather | bytes 6912 | tf_op jit(solution)/shard_map/all_gather | solution.py:126
  57.7 4.2 collective-permute-start.6
  63.5 15.8 %fusion.250 = (f32[32,32]{1,0:T(8,128)S(1)}, f32[1,32,32,384]{3,2,1,0:T(8,128)S(1)}) fusion(f32[384]{0:T(512)S(1)} %get-tuple-element.174, f32[384]{0:T(512)S(1)} %get-tuple-element.117, bf16[1,38,3,384]{3,2,1,0:T(4,128)(2,1)S(1)} %collective-permute-done.3, bf16[1,38,32,384]{3,2,1,0:T(8,128)(2,1)S(1)} %get-tuple-element.218, ...), kind=kLoop, calls=%fused_computation.649 | loop fusion | flops 107740160 | bytes 8267776 | tf_op jit(solution)/shard_map/reduce_sum | solution.py:48
  80.0 16.4 %fusion.248 = (f32[32,32]{1,0:T(8,128)S(1)}, f32[1,32,32,384]{3,2,1,0:T(8,128)S(1)}) fusion(f32[384]{0:T(512)S(1)} %get-tuple-element.171, f32[384]{0:T(512)S(1)} %get-tuple-element.146, bf16[1,38,3,384]{3,2,1,0:T(4,128)(2,1)S(1)} %collective-permute-done.7, bf16[1,38,32,384]{3,2,1,0:T(8,128)(2,1)S(1)} %get-tuple-element.214, ...), kind=kLoop, calls=%fused_computation.648 | loop fusion | flops 107740160 | bytes 8267776 | tf_op jit(solution)/shard_map/reduce_sum | solution.py:48
  98.4 6.7 multiply_convert_fusion
  105.1 33.4 %all-gather.6.cloned.1.call-done = bf16[2,1536,384]{2,1,0:T(8,128)(2,1)} async-done(((bf16[2,192,384]{2,1,0:T(8,128)(2,1)}), bf16[2,1536,384]{2,1,0:T(8,128)(2,1)}) %all-gather.6.cloned.1.call-update) | async-done | bytes 2359312 | tf_op jit(solution)/shard_map/all_gather | solution.py:127
  138.5 5.4 fusion.153
  143.9 4.3 fusion.4
  167.4 3.6 fusion.149
  171.1 4.4 stack.220
  175.5 5.2 fusion.258
  181.8 5.1 fusion.257
  189.1 4.3 collective-permute-start.8
  197.9 19.3 %all-reduce = f32[1536]{0:T(1024)S(1)} all-reduce(f32[1536]{0:T(1024)S(1)} %convert_reduce_fusion.1), channel_id=3, replica_groups=mesh['dp'=8,'row'=4,'col'=8] {'dp'}, use_global_device_ids=true, to_apply=%region_9.0.clone | all-reduce | flops 1536 | bytes 12288
  217.3 54.5 %psum.43 = f32[192]{0:T(256)S(1)} all-reduce(f32[192]{0:T(256)S(1)} %dynamic-slice.1), channel_id=1, replica_groups=mesh['dp'=8,'row'=4,'col'=8] {'row','col'}, use_global_device_ids=true, to_apply=%region_10.0 | all-reduce | flops 192 | bytes 1536 | tf_op jit(solution)/shard_map/psum | solution.py:162
  271.8 77.7 %all-reduce.1 = (f32[2,384]{1,0:T(2,128)S(1)}, f32[3,384]{1,0:T(4,128)S(1)}) all-reduce(f32[2,384]{1,0:T(2,128)S(1)} %pad_maximum_fusion.11, f32[3,384]{1,0:T(4,128)S(1)} %pad_maximum_fusion.10), channel_id=1, replica_groups=mesh['dp'=8,'row'=4,'col'=8] {'dp','row','col'}, use_global_device_ids=true, to_apply=%region_65.0 | all-reduce | flops 1920 | bytes 15360 | tf_op jit(solution)/shard_map/psum | solution.py:156
  350.7 6.3 convolution_add_fusion.1
  364.1 56.6 %all-reduce.6.cloned.1.call-done = f32[49,384]{1,0:T(8,128)} async-done(((f32[49,384]{1,0:T(8,128)}), f32[49,384]{1,0:T(8,128)}) %all-reduce.6.cloned.1.call-update) | async-done | bytes 75280 | tf_op jit(solution)/shard_map/psum | solution.py:156
  423.0 79.1 %reduce-scatter.5.cloned.1.call-done = f32[192,384]{1,0:T(8,128)} async-done(((f32[1536,384]{1,0:T(8,128)}), f32[192,384]{1,0:T(8,128)}) %reduce-scatter.5.cloned.1.call-update) | async-done | bytes 294928 | tf_op jit(solution)/shard_map/reduce_scatter | solution.py:160
  502.1 85.7 %reduce-scatter.3.cloned.1.call-done = f32[384,192]{0,1:T(8,128)} async-done(((f32[384,1536]{0,1:T(8,128)}), f32[384,192]{0,1:T(8,128)}) %reduce-scatter.3.cloned.1.call-update) | async-done | bytes 294928 | tf_op jit(solution)/shard_map/reduce_scatter | solution.py:158
  587.9 17.0 %convert_add_fusion.2 = f32[1,32,32,384]{3,2,1,0:T(8,128)} fusion(bf16[1,32,32,384]{3,2,1,0:T(8,128)(2,1)} %param.11, bf16[1,32,32,384]{3,2,1,0:T(8,128)(2,1)S(1)} %multiply_convert_fusion.2, bf16[1,3,32,384]{3,2,1,0:T(8,128)(2,1)S(1)} %collective-permute-done.9, bf16[1,3,32,384]{3,2,1,0:T(8,128)(2,1)S(1)} %collective-permute-done.8, ...), kind=kLoop, calls=%fused_computation.342 | loop fusion | flops 60555264 | bytes 36398592 | tf_op jit(solution)/shard_map/add | solution.py:117
  604.9 214.2 %all-reduce.8.cloned.1.call-done = (f32[384,192]{0,1:T(8,128)}, f32[192,384]{1,0:T(8,128)}) async-done(((f32[384,192]{0,1:T(8,128)}, f32[192,384]{1,0:T(8,128)}), (f32[384,192]{0,1:T(8,128)}, f32[192,384]{1,0:T(8,128)})) %all-reduce.8.cloned.1.call-update) | async-done | bytes 589840 | tf_op jit(solution)/shard_map/psum | solution.py:162
  (272 shorter events, 65.9 us)
Async XLA Ops:
  7.2 91.2 %all-gather.4.cloned.1.call-start = ((), (), s32[]{:S(2)}) async-start(), calls=%async_computation.2 | async-start | bytes 2654208 | tf_op jit(solution)/shard_map/all_gather | solution.py:125
  7.9 130.6 %all-gather.6.cloned.1.call-start = ((), (), s32[]{:S(2)}) async-start(), calls=%async_computation.3 | async-start | bytes 2654208 | tf_op jit(solution)/shard_map/all_gather | solution.py:127
  8.9 42.8 %collective-permute-start = (bf16[1,3,32,384]{3,2,1,0:T(8,128)(2,1)S(1)}, bf16[1,3,32,384]{3,2,1,0:T(8,128)(2,1)S(1)}, u32[]{:S(2)}, u32[]{:S(2)}) collective-permute-start(bf16[1,3,32,384]{3,2,1,0:T(8,128)(2,1)S(1)} %get-tuple-element.210), channel_id=1, source_target_pairs={{0,8},{8,16},{16,24},{1,9},{9,17},{17,25},{2,10},{10,18},{18,26},{... | collective-permute-start | bytes 221192 | tf_op jit(solution)/shard_map/ppermute | solution.py:19
  13.5 38.6 %collective-permute-start.1 = (bf16[1,3,32,384]{3,2,1,0:T(8,128)(2,1)S(1)}, bf16[1,3,32,384]{3,2,1,0:T(8,128)(2,1)S(1)}, u32[]{:S(2)}, u32[]{:S(2)}) collective-permute-start(bf16[1,3,32,384]{3,2,1,0:T(8,128)(2,1)S(1)} %get-tuple-element.209), channel_id=1, source_target_pairs={{8,0},{16,8},{24,16},{9,1},{17,9},{25,17},{10,2},{18,10},{26,18},{... | collective-permute-start | bytes 221192 | tf_op jit(solution)/shard_map/ppermute | solution.py:20
  16.4 40.7 %collective-permute-start.4 = (bf16[1,3,32,384]{3,2,1,0:T(8,128)(2,1)S(1)}, bf16[1,3,32,384]{3,2,1,0:T(8,128)(2,1)S(1)}, u32[]{:S(2)}, u32[]{:S(2)}) collective-permute-start(bf16[1,3,32,384]{3,2,1,0:T(8,128)(2,1)S(1)} %get-tuple-element.205), channel_id=1, source_target_pairs={{0,8},{8,16},{16,24},{1,9},{9,17},{17,25},{2,10},{10,18},{18,26},{... | collective-permute-start | bytes 221192 | tf_op jit(solution)/shard_map/ppermute | solution.py:19
  20.0 37.5 %collective-permute-start.5 = (bf16[1,3,32,384]{3,2,1,0:T(8,128)(2,1)S(1)}, bf16[1,3,32,384]{3,2,1,0:T(8,128)(2,1)S(1)}, u32[]{:S(2)}, u32[]{:S(2)}) collective-permute-start(bf16[1,3,32,384]{3,2,1,0:T(8,128)(2,1)S(1)} %get-tuple-element.204), channel_id=1, source_target_pairs={{8,0},{16,8},{24,16},{9,1},{17,9},{25,17},{10,2},{18,10},{26,18},{... | collective-permute-start | bytes 221192 | tf_op jit(solution)/shard_map/ppermute | solution.py:20
  22.0 398.7 %all-reduce.6.cloned.1.call-start = ((), (), s32[]{:S(2)}) async-start(), calls=%async_computation.6 | async-start | bytes 172032 | tf_op jit(solution)/shard_map/psum | solution.py:156
  25.9 53.8 %copy-start.19 = (f32[384]{0:T(512)}, f32[384]{0:T(512)S(1)}, u32[]{:S(2)}) copy-start(f32[384]{0:T(512)S(1)} %get-tuple-element.90) | copy-start | bytes 4612
  25.9 53.8 %copy-start.20 = (f32[384]{0:T(512)}, f32[384]{0:T(512)S(1)}, u32[]{:S(2)}) copy-start(f32[384]{0:T(512)S(1)} %get-tuple-element.91) | copy-start | bytes 4612
  25.9 53.8 %copy-start.21 = (f32[384]{0:T(512)}, f32[384]{0:T(512)S(1)}, u32[]{:S(2)}) copy-start(f32[384]{0:T(512)S(1)} %get-tuple-element.92) | copy-start | bytes 4612
  52.3 11.2 %collective-permute-start.2 = (bf16[1,38,3,384]{3,2,1,0:T(4,128)(2,1)S(1)}, bf16[1,38,3,384]{3,2,1,0:T(4,128)(2,1)S(1)}, u32[]{:S(2)}, u32[]{:S(2)}) collective-permute-start(bf16[1,38,3,384]{3,2,1,0:T(4,128)(2,1)S(1)} %get-tuple-element.194), channel_id=1, source_target_pairs={{0,1},{1,2},{2,3},{3,4},{4,5},{5,6},{6,7},{8,9},{9,10},{10,11},{11... | collective-permute-start | bytes 262664 | tf_op jit(solution)/shard_map/ppermute | solution.py:19
  55.8 7.7 collective-permute-start.3
  57.7 21.9 %collective-permute-start.6 = (bf16[1,38,3,384]{3,2,1,0:T(4,128)(2,1)S(1)}, bf16[1,38,3,384]{3,2,1,0:T(4,128)(2,1)S(1)}, u32[]{:S(2)}, u32[]{:S(2)}) collective-permute-start(bf16[1,38,3,384]{3,2,1,0:T(4,128)(2,1)S(1)} %get-tuple-element.192), channel_id=1, source_target_pairs={{0,1},{1,2},{2,3},{3,4},{4,5},{5,6},{6,7},{8,9},{9,10},{10,11},{11... | collective-permute-start | bytes 262664 | tf_op jit(solution)/shard_map/ppermute | solution.py:19
  62.0 17.7 %collective-permute-start.7 = (bf16[1,38,3,384]{3,2,1,0:T(4,128)(2,1)S(1)}, bf16[1,38,3,384]{3,2,1,0:T(4,128)(2,1)S(1)}, u32[]{:S(2)}, u32[]{:S(2)}) collective-permute-start(bf16[1,38,3,384]{3,2,1,0:T(4,128)(2,1)S(1)} %get-tuple-element.193), channel_id=1, source_target_pairs={{1,0},{2,1},{3,2},{4,3},{5,4},{6,5},{7,6},{9,8},{10,9},{11,10},{12... | collective-permute-start | bytes 262664 | tf_op jit(solution)/shard_map/ppermute | solution.py:20
  175.5 326.6 %reduce-scatter.5.cloned.1.call-start = ((), (), s32[]{:S(2)}) async-start(), calls=%async_computation.5 | async-start | bytes 2654208 | tf_op jit(solution)/shard_map/reduce_scatter | solution.py:160
  180.7 407.1 %reduce-scatter.3.cloned.1.call-start = ((), (), s32[]{:S(2)}) async-start(), calls=%async_computation.4 | async-start | bytes 2654208 | tf_op jit(solution)/shard_map/reduce_scatter | solution.py:158
  187.0 632.0 %all-reduce.8.cloned.1.call-start = ((), (), s32[]{:S(2)}) async-start(), calls=%async_computation.7 | async-start | bytes 1179648 | tf_op jit(solution)/shard_map/psum | solution.py:162
  189.1 171.2 %collective-permute-start.8 = (bf16[1,3,32,384]{3,2,1,0:T(8,128)(2,1)S(1)}, bf16[1,3,32,384]{3,2,1,0:T(8,128)(2,1)S(1)}, u32[]{:S(2)}, u32[]{:S(2)}) collective-permute-start(bf16[1,3,32,384]{3,2,1,0:T(8,128)(2,1)S(1)} %get-tuple-element.199), channel_id=1, source_target_pairs={{0,8},{8,16},{16,24},{1,9},{9,17},{17,25},{2,10},{10,18},{18,26},{... | collective-permute-start | bytes 221192 | tf_op jit(solution)/shard_map/ppermute | solution.py:19
  193.4 157.2 %copy-start.13 = (bf16[1,32,32,384]{3,2,1,0:T(8,128)(2,1)S(1)}, bf16[1,32,32,384]{3,2,1,0:T(8,128)(2,1)}, u32[]{:S(2)}) copy-start(bf16[1,32,32,384]{3,2,1,0:T(8,128)(2,1)} %get-tuple-element.224) | copy-start | bytes 2359300
  193.5 157.2 %copy-start.57 = (f32[1536]{0:T(1024)S(1)}, f32[1536]{0:T(1024)}, u32[]{:S(2)}) copy-start(f32[1536]{0:T(1024)} %get-tuple-element.169) | copy-start | bytes 18436
  193.5 157.2 %copy-start.59 = (f32[384]{0:T(512)S(1)}, f32[384]{0:T(512)}, u32[]{:S(2)}) copy-start(f32[384]{0:T(512)} %get-tuple-element.172) | copy-start | bytes 4612
  193.5 166.9 %collective-permute-start.9 = (bf16[1,3,32,384]{3,2,1,0:T(8,128)(2,1)S(1)}, bf16[1,3,32,384]{3,2,1,0:T(8,128)(2,1)S(1)}, u32[]{:S(2)}, u32[]{:S(2)}) collective-permute-start(bf16[1,3,32,384]{3,2,1,0:T(8,128)(2,1)S(1)} %get-tuple-element.200), channel_id=1, source_target_pairs={{8,0},{16,8},{24,16},{9,1},{17,9},{25,17},{10,2},{18,10},{26,18},{... | collective-permute-start | bytes 221192 | tf_op jit(solution)/shard_map/ppermute | solution.py:20
  360.5 61.8 %collective-permute-start.10 = (bf16[1,38,3,384]{3,2,1,0:T(4,128)(2,1)S(1)}, bf16[1,38,3,384]{3,2,1,0:T(4,128)(2,1)S(1)}, u32[]{:S(2)}, u32[]{:S(2)}) collective-permute-start(bf16[1,38,3,384]{3,2,1,0:T(4,128)(2,1)S(1)} %get-tuple-element.190), channel_id=1, source_target_pairs={{0,1},{1,2},{2,3},{3,4},{4,5},{5,6},{6,7},{8,9},{9,10},{10,11},{11... | collective-permute-start | bytes 262664 | tf_op jit(solution)/shard_map/ppermute | solution.py:19
  362.8 59.5 %collective-permute-start.11 = (bf16[1,38,3,384]{3,2,1,0:T(4,128)(2,1)S(1)}, bf16[1,38,3,384]{3,2,1,0:T(4,128)(2,1)S(1)}, u32[]{:S(2)}, u32[]{:S(2)}) collective-permute-start(bf16[1,38,3,384]{3,2,1,0:T(4,128)(2,1)S(1)} %get-tuple-element.191), channel_id=1, source_target_pairs={{1,0},{2,1},{3,2},{4,3},{5,4},{6,5},{7,6},{9,8},{10,9},{11,10},{12... | collective-permute-start | bytes 262664 | tf_op jit(solution)/shard_map/ppermute | solution.py:20
  (59 other events, 2060.6 us)
Sparse Core Ops, SparseCore 0:
  10.6 64.3 all-gather.3
  77.6 60.8 all-gather.5
  175.6 245.0 all-reduce.5
  424.7 77.4 reduce-scatter.4
  506.1 81.7 reduce-scatter.2
  590.4 228.6 all-reduce.7
where the time goes:
time: 831 us; the launch traced here: 829 us
  waiting for transfers between devices  470 us (57%)
  blocking collectives  171 us (21%)
  other arithmetic  92.2 us (11%)
  matrix products  34.8 us (4%)
  starting transfers between devices  32.8 us (4%)
  between operations  16.4 us (2%)
  local copies, waits for them, and re-layouts  12.1 us (1%)
    psum x1, waiting for transfers between devices, on_device(): shares = lax.psum((owned[0], owned[1], owned[2]), ('row', 'col'))  214 us
    reduce_scatter x1, waiting for transfers between devices, on_device(): lax.psum_scatter(large_grads[0], 'dp', scatter_dimension=1, tiled=True)  85.7 us
    reduce_scatter x1, waiting for transfers between devices, on_device(): lax.psum_scatter(large_grads[2], 'dp', scatter_dimension=0, tiled=True)  79.1 us
    psum x1, blocking collectives, on_device(): lax.psum((minor_grads[0], minor_grads[1], minor_grads[2]), ('dp', 'row',...  77.7 us
    psum x1, waiting for transfers between devices, on_device(): lax.psum((minor_grads[0], minor_grads[1], minor_grads[2]), ('dp', 'row',...  56.6 us
    psum x1, blocking collectives, on_device(): shares = lax.psum((owned[0], owned[1], owned[2]), ('row', 'col'))  54.5 us
    all_gather x1, waiting for transfers between devices, on_device(): lax.all_gather(weight_out, 'dp', axis=1, tiled=True)  33.4 us
    reduce_sum x2, other arithmetic, forward(): centered = convolved - jnp.mean(convolved, axis=-1, keepdims=True)  32.2 us
  transfers between devices with their start and end apart: 18, of which 5 were waited for; matrix products, arithmetic and copies ran while one was open for 12% of the time, Pallas kernels for 0%

commit v1 on v0

--- a/solution.py
+++ b/solution.py
@@ -7,6 +7,7 @@
 EPSILON = 1e-06
 ROOT_HALF = 0.7071067811865476
 INV_ROOT_TWO_PI = 0.3989422804014327
+pack_the_shards = lambda unit: lax.psum(lax.psum(unit, ("row", "col")), "dp")
 
 
 def with_halo(value, sides, width):
@@ -153,7 +154,7 @@
     )
     grad_pad = with_halo(conv_grad, (("row", 1), ("col", 2)), margin)
     in_grad = input_gradient(cotangent, grad_pad, kernels[1])
-    minor_sums = lax.psum((minor_grads[0], minor_grads[1], minor_grads[2]), ("dp", "row", "col"))
+    minor_sums = pack_the_shards((minor_grads[0], minor_grads[1], minor_grads[2]))
     owned = (
         lax.psum_scatter(large_grads[0], "dp", scatter_dimension=1, tiled=True),
         lax.psum_scatter(large_grads[1], "dp", scatter_dimension=0, tiled=True),

time: 831 us -> 736 us (0.89)
  waiting for transfers between devices: 470 us -> 382 us
  blocking collectives: 171 us -> 162 us
    reduce_scatter x1, waiting for transfers between devices: 79.1 us -> 0.02 us  [on_device(): lax.psum_scatter(large_grads[2], 'dp', scatter_dimension=0, tiled=True)]
    psum x1, blocking collectives: 77.7 us -> 17.5 us  [lax.psum(lax.psum(unit, ('row', 'col')), 'dp')]
    psum x1, blocking collectives: 54.5 us -> 106 us  [on_device(): shares = lax.psum((owned[0], owned[1], owned[2]), ('row', 'col'))]
    reduce_scatter x1, waiting for transfers between devices: 85.7 us -> 54.2 us  [on_device(): lax.psum_scatter(large_grads[0], 'dp', scatter_dimension=1, tiled=True)]
    psum x1, waiting for transfers between devices: 56.6 us -> 78.8 us  [lax.psum(lax.psum(unit, ('row', 'col')), 'dp')]
  transfers between devices with their start and end apart: 18 -> 18, of which waited for: 5 -> 4; matrix products, arithmetic and copies ran while one was open for 12% -> 17% of each run, Pallas kernels for 0% -> 0%
where the time goes in v1:
time: 736 us; the launch traced here: 731 us
  waiting for transfers between devices  382 us (52%)
  blocking collectives  162 us (22%)
  other arithmetic  91.7 us (12%)
  matrix products  33.4 us (5%)
  starting transfers between devices  32.8 us (4%)
  between operations  17.2 us (2%)
  local copies, waits for them, and re-layouts  11.8 us (2%)
    psum x1, waiting for transfers between devices, on_device(): shares = lax.psum((owned[0], owned[1], owned[2]), ('row', 'col'))  215 us
    psum x1, blocking collectives, on_device(): shares = lax.psum((owned[0], owned[1], owned[2]), ('row', 'col'))  106 us
    psum x1, waiting for transfers between devices, lax.psum(lax.psum(unit, ('row', 'col')), 'dp')  78.8 us
    reduce_scatter x1, waiting for transfers between devices, on_device(): lax.psum_scatter(large_grads[0], 'dp', scatter_dimension=1, tiled=True)  54.2 us
    all_gather x1, waiting for transfers between devices, on_device(): lax.all_gather(weight_out, 'dp', axis=1, tiled=True)  32.6 us
    reduce_sum x2, other arithmetic, forward(): centered = convolved - jnp.mean(convolved, axis=-1, keepdims=True)  31.5 us
    ppermute x6, starting transfers between devices, with_halo(): before = lax.ppermute(last, axis, up)  22.1 us
    all_gather x1, blocking collectives, on_device(): lax.all_gather(bias_in, 'dp', axis=1, tiled=True)  19.5 us
  transfers between devices with their start and end apart: 18, of which 4 were waited for; matrix products, arithmetic and copies ran while one was open for 17% of the time, Pallas kernels for 0%

profile of v1, /device:TPU:1, one launch (start us, length us, event | category | flops | bytes accessed | tf_op | source)
XLA Modules:
  0.0 731.1 jit_solution(2152991851782614525)
XLA Ops:
  8.9 4.6 collective-permute-start
  16.4 3.6 collective-permute-start.4
  30.6 19.5 %all-gather = bf16[8,192,2]{1,2,0:T(2,128)(2,1)S(1)} all-gather(bf16[1,192,2]{1,2,0:T(2,128)(2,1)S(1)} %bitcast.59), channel_id=1, replica_groups=mesh['dp'=8,'row'=4,'col'=8] {'dp'}, dimensions={0}, use_global_device_ids=true | all-gather | bytes 6912 | tf_op jit(solution)/shard_map/all_gather | solution.py:127
  53.4 3.5 collective-permute-start.2
  58.8 4.2 collective-permute-start.6
  64.5 15.8 %fusion.250 = (f32[32,32]{1,0:T(8,128)S(1)}, f32[1,32,32,384]{3,2,1,0:T(8,128)S(1)}) fusion(f32[384]{0:T(512)S(1)} %get-tuple-element.174, f32[384]{0:T(512)S(1)} %get-tuple-element.117, bf16[1,38,3,384]{3,2,1,0:T(4,128)(2,1)S(1)} %collective-permute-done.3, bf16[1,38,32,384]{3,2,1,0:T(8,128)(2,1)S(1)} %get-tuple-element.222, ...), kind=kLoop, calls=%fused_computation.649 | loop fusion | flops 107740160 | bytes 8267776 | tf_op jit(solution)/shard_map/reduce_sum | solution.py:49
  81.3 15.7 %fusion.248 = (f32[32,32]{1,0:T(8,128)S(1)}, f32[1,32,32,384]{3,2,1,0:T(8,128)S(1)}) fusion(f32[384]{0:T(512)S(1)} %copy-done.111, f32[384]{0:T(512)S(1)} %get-tuple-element.146, bf16[1,38,3,384]{3,2,1,0:T(4,128)(2,1)S(1)} %collective-permute-done.7, bf16[1,38,32,384]{3,2,1,0:T(8,128)(2,1)S(1)} %get-tuple-element.218, f32[384]{0:T(512)S(1)} %get-tuple-element.127, ...), kind=kLoop, calls=%fused_computation.648 | loop fusion | flops 107740160 | bytes 8267776 | tf_op jit(solution)/shard_map/reduce_sum | solution.py:49
  99.2 6.7 multiply_convert_fusion
  105.9 32.6 %all-gather.6.cloned.1.call-done = bf16[2,1536,384]{2,1,0:T(8,128)(2,1)} async-done(((bf16[2,192,384]{2,1,0:T(8,128)(2,1)}), bf16[2,1536,384]{2,1,0:T(8,128)(2,1)}) %all-gather.6.cloned.1.call-update) | async-done | bytes 2359312 | tf_op jit(solution)/shard_map/all_gather | solution.py:128
  138.5 5.6 fusion.153
  144.1 3.3 fusion.258
  147.7 6.2 fusion.4
  161.8 4.2 fusion.149
  166.9 4.3 collective-permute-start.8
  173.8 19.4 %all-reduce = f32[1536]{0:T(1024)S(1)} all-reduce(f32[1536]{0:T(1024)S(1)} %convert_reduce_fusion.1), channel_id=3, replica_groups=mesh['dp'=8,'row'=4,'col'=8] {'dp'}, use_global_device_ids=true, to_apply=%region_9.0.clone | all-reduce | flops 1536 | bytes 12288
  193.3 106.0 %all-reduce.1 = (f32[192]{0:T(256)}, f32[2,384]{1,0:T(2,128)S(1)}, f32[3,384]{1,0:T(4,128)S(1)}) all-reduce(f32[192]{0:T(256)S(1)} %dynamic-slice.1, f32[2,384]{1,0:T(2,128)S(1)} %pad_maximum_fusion.11, f32[3,384]{1,0:T(4,128)S(1)} %pad_maximum_fusion.10), channel_id=1, replica_groups=mesh['dp'=8,'row'=4,'col'=8] {'row','col'}, use_global_device_ids=true, to_apply=%region_10.0 | all-reduce | flops 2112 | bytes 16896 | tf_op jit(solution)/shard_map/psum | solution.py:163
  299.4 17.5 %all-reduce.3 = (f32[2,384]{1,0:T(2,128)}, f32[3,384]{1,0:T(4,128)S(1)}) all-reduce(f32[2,384]{1,0:T(2,128)S(1)} %get-tuple-element.181, f32[3,384]{1,0:T(4,128)S(1)} %get-tuple-element.182), channel_id=1, replica_groups=mesh['dp'=8,'row'=4,'col'=8] {'dp'}, use_global_device_ids=true, to_apply=%region_67.0 | all-reduce | flops 1920 | bytes 15360 | tf_op jit(solution)/shard_map/psum | solution.py:10
  319.4 3.3 fusion.257
  323.0 5.5 convolution_add_fusion.1
  347.6 4.4 stack.220
  354.0 54.2 %reduce-scatter.3.cloned.1.call-done = f32[384,192]{0,1:T(8,128)} async-done(((f32[384,1536]{0,1:T(8,128)}), f32[384,192]{0,1:T(8,128)}) %reduce-scatter.3.cloned.1.call-update) | async-done | bytes 294928 | tf_op jit(solution)/shard_map/reduce_scatter | solution.py:159
  408.6 16.6 %convert_add_fusion.2 = f32[1,32,32,384]{3,2,1,0:T(8,128)} fusion(bf16[1,32,32,384]{3,2,1,0:T(8,128)(2,1)} %param.11, bf16[1,32,32,384]{3,2,1,0:T(8,128)(2,1)S(1)} %multiply_convert_fusion.2, bf16[1,3,32,384]{3,2,1,0:T(8,128)(2,1)S(1)} %collective-permute-done.9, bf16[1,3,32,384]{3,2,1,0:T(8,128)(2,1)S(1)} %collective-permute-done.8, ...), kind=kLoop, calls=%fused_computation.342 | loop fusion | flops 60555264 | bytes 36398592 | tf_op jit(solution)/shard_map/add | solution.py:118
  425.3 215.2 %all-reduce.9.cloned.1.call-done = (f32[384,192]{0,1:T(8,128)}, f32[192,384]{1,0:T(8,128)}, f32[49,384]{1,0:T(8,128)}) async-done(((f32[384,192]{0,1:T(8,128)}, f32[192,384]{1,0:T(8,128)}, f32[49,384]{1,0:T(8,128)}), (f32[384,192]{0,1:T(8,128)}, f32[192,384]{1,0:T(8,128)}, f32[49,384]{1,0:T(8,128)})) %all-reduce.9.cloned.1.call-update) | async-done | bytes 665104 | tf_op jit(solution)/shard_map/psum | solution.py:163
  643.9 78.8 %all-reduce.7.cloned.1.call-done = f32[49,384]{1,0:T(8,128)} async-done(((f32[49,384]{1,0:T(8,128)}), f32[49,384]{1,0:T(8,128)}) %all-reduce.7.cloned.1.call-update) | async-done | bytes 75280 | tf_op jit(solution)/shard_map/psum | solution.py:10
  (388 shorter events, 63.2 us)
Async XLA Ops:
  7.2 92.0 %all-gather.4.cloned.1.call-start = ((), (), s32[]{:S(2)}) async-start(), calls=%async_computation.2 | async-start | bytes 2654208 | tf_op jit(solution)/shard_map/all_gather | solution.py:126
  7.9 130.6 %all-gather.6.cloned.1.call-start = ((), (), s32[]{:S(2)}) async-start(), calls=%async_computation.3 | async-start | bytes 2654208 | tf_op jit(solution)/shard_map/all_gather | solution.py:128
  8.9 43.8 %collective-permute-start = (bf16[1,3,32,384]{3,2,1,0:T(8,128)(2,1)S(1)}, bf16[1,3,32,384]{3,2,1,0:T(8,128)(2,1)S(1)}, u32[]{:S(2)}, u32[]{:S(2)}) collective-permute-start(bf16[1,3,32,384]{3,2,1,0:T(8,128)(2,1)S(1)} %get-tuple-element.214), channel_id=1, source_target_pairs={{0,8},{8,16},{16,24},{1,9},{9,17},{17,25},{2,10},{10,18},{18,26},{... | collective-permute-start | bytes 221192 | tf_op jit(solution)/shard_map/ppermute | solution.py:20
  13.5 39.7 %collective-permute-start.1 = (bf16[1,3,32,384]{3,2,1,0:T(8,128)(2,1)S(1)}, bf16[1,3,32,384]{3,2,1,0:T(8,128)(2,1)S(1)}, u32[]{:S(2)}, u32[]{:S(2)}) collective-permute-start(bf16[1,3,32,384]{3,2,1,0:T(8,128)(2,1)S(1)} %get-tuple-element.213), channel_id=1, source_target_pairs={{8,0},{16,8},{24,16},{9,1},{17,9},{25,17},{10,2},{18,10},{26,18},{... | collective-permute-start | bytes 221192 | tf_op jit(solution)/shard_map/ppermute | solution.py:21
  16.4 41.8 %collective-permute-start.4 = (bf16[1,3,32,384]{3,2,1,0:T(8,128)(2,1)S(1)}, bf16[1,3,32,384]{3,2,1,0:T(8,128)(2,1)S(1)}, u32[]{:S(2)}, u32[]{:S(2)}) collective-permute-start(bf16[1,3,32,384]{3,2,1,0:T(8,128)(2,1)S(1)} %get-tuple-element.209), channel_id=1, source_target_pairs={{0,8},{8,16},{16,24},{1,9},{9,17},{17,25},{2,10},{10,18},{18,26},{... | collective-permute-start | bytes 221192 | tf_op jit(solution)/shard_map/ppermute | solution.py:20
  20.0 38.6 %collective-permute-start.5 = (bf16[1,3,32,384]{3,2,1,0:T(8,128)(2,1)S(1)}, bf16[1,3,32,384]{3,2,1,0:T(8,128)(2,1)S(1)}, u32[]{:S(2)}, u32[]{:S(2)}) collective-permute-start(bf16[1,3,32,384]{3,2,1,0:T(8,128)(2,1)S(1)} %get-tuple-element.208), channel_id=1, source_target_pairs={{8,0},{16,8},{24,16},{9,1},{17,9},{25,17},{10,2},{18,10},{26,18},{... | collective-permute-start | bytes 221192 | tf_op jit(solution)/shard_map/ppermute | solution.py:21
  22.0 332.0 %reduce-scatter.5.cloned.1.call-start = ((), (), s32[]{:S(2)}) async-start(), calls=%async_computation.5 | async-start | bytes 2654208 | tf_op jit(solution)/shard_map/reduce_scatter | solution.py:161
  23.0 57.8 %copy-start.19 = (f32[384]{0:T(512)}, f32[384]{0:T(512)S(1)}, u32[]{:S(2)}) copy-start(f32[384]{0:T(512)S(1)} %get-tuple-element.114) | copy-start | bytes 4612
  23.0 57.8 %copy-start.21 = (f32[384]{0:T(512)}, f32[384]{0:T(512)S(1)}, u32[]{:S(2)}) copy-start(f32[384]{0:T(512)S(1)} %get-tuple-element.115) | copy-start | bytes 4612
  23.0 57.8 %copy-start.23 = (f32[384]{0:T(512)}, f32[384]{0:T(512)S(1)}, u32[]{:S(2)}) copy-start(f32[384]{0:T(512)S(1)} %get-tuple-element.116) | copy-start | bytes 4612
  24.0 56.8 %copy-start.25 = (f32[384]{0:T(512)}, f32[384]{0:T(512)S(1)}, u32[]{:S(2)}) copy-start(f32[384]{0:T(512)S(1)} %get-tuple-element.127) | copy-start | bytes 4612
  53.4 11.1 %collective-permute-start.2 = (bf16[1,38,3,384]{3,2,1,0:T(4,128)(2,1)S(1)}, bf16[1,38,3,384]{3,2,1,0:T(4,128)(2,1)S(1)}, u32[]{:S(2)}, u32[]{:S(2)}) collective-permute-start(bf16[1,38,3,384]{3,2,1,0:T(4,128)(2,1)S(1)} %get-tuple-element.198), channel_id=1, source_target_pairs={{0,1},{1,2},{2,3},{3,4},{4,5},{5,6},{6,7},{8,9},{9,10},{10,11},{11... | collective-permute-start | bytes 262664 | tf_op jit(solution)/shard_map/ppermute | solution.py:20
  56.9 7.6 %collective-permute-start.3 = (bf16[1,38,3,384]{3,2,1,0:T(4,128)(2,1)S(1)}, bf16[1,38,3,384]{3,2,1,0:T(4,128)(2,1)S(1)}, u32[]{:S(2)}, u32[]{:S(2)}) collective-permute-start(bf16[1,38,3,384]{3,2,1,0:T(4,128)(2,1)S(1)} %get-tuple-element.199), channel_id=1, source_target_pairs={{1,0},{2,1},{3,2},{4,3},{5,4},{6,5},{7,6},{9,8},{10,9},{11,10},{12... | collective-permute-start | bytes 262664 | tf_op jit(solution)/shard_map/ppermute | solution.py:21
  58.8 21.9 %collective-permute-start.6 = (bf16[1,38,3,384]{3,2,1,0:T(4,128)(2,1)S(1)}, bf16[1,38,3,384]{3,2,1,0:T(4,128)(2,1)S(1)}, u32[]{:S(2)}, u32[]{:S(2)}) collective-permute-start(bf16[1,38,3,384]{3,2,1,0:T(4,128)(2,1)S(1)} %get-tuple-element.196), channel_id=1, source_target_pairs={{0,1},{1,2},{2,3},{3,4},{4,5},{5,6},{6,7},{8,9},{9,10},{10,11},{11... | collective-permute-start | bytes 262664 | tf_op jit(solution)/shard_map/ppermute | solution.py:20
  63.0 17.8 %collective-permute-start.7 = (bf16[1,38,3,384]{3,2,1,0:T(4,128)(2,1)S(1)}, bf16[1,38,3,384]{3,2,1,0:T(4,128)(2,1)S(1)}, u32[]{:S(2)}, u32[]{:S(2)}) collective-permute-start(bf16[1,38,3,384]{3,2,1,0:T(4,128)(2,1)S(1)} %get-tuple-element.197), channel_id=1, source_target_pairs={{1,0},{2,1},{3,2},{4,3},{5,4},{6,5},{7,6},{9,8},{10,9},{11,10},{12... | collective-permute-start | bytes 262664 | tf_op jit(solution)/shard_map/ppermute | solution.py:21
  147.4 260.8 %reduce-scatter.3.cloned.1.call-start = ((), (), s32[]{:S(2)}) async-start(), calls=%async_computation.4 | async-start | bytes 2654208 | tf_op jit(solution)/shard_map/reduce_scatter | solution.py:159
  166.9 176.1 %collective-permute-start.8 = (bf16[1,3,32,384]{3,2,1,0:T(8,128)(2,1)}, bf16[1,3,32,384]{3,2,1,0:T(8,128)(2,1)S(1)}, u32[]{:S(2)}, u32[]{:S(2)}) collective-permute-start(bf16[1,3,32,384]{3,2,1,0:T(8,128)(2,1)} %get-tuple-element.203), channel_id=1, source_target_pairs={{0,8},{8,16},{16,24},{1,9},{9,17},{17,25},{2,10},{10,18},{18,26},{... | collective-permute-start | bytes 221192 | tf_op jit(solution)/shard_map/ppermute | solution.py:20
  171.2 146.3 %copy-start.4 = (bf16[1,35,32,384]{3,2,1,0:T(8,128)(2,1)S(1)}, bf16[1,35,32,384]{3,2,1,0:T(8,128)(2,1)}, u32[]{:S(2)}) copy-start(bf16[1,35,32,384]{3,2,1,0:T(8,128)(2,1)} %copy-done.3) | copy-start | bytes 2580484
  171.2 171.8 %collective-permute-start.9 = (bf16[1,3,32,384]{3,2,1,0:T(8,128)(2,1)}, bf16[1,3,32,384]{3,2,1,0:T(8,128)(2,1)S(1)}, u32[]{:S(2)}, u32[]{:S(2)}) collective-permute-start(bf16[1,3,32,384]{3,2,1,0:T(8,128)(2,1)} %get-tuple-element.204), channel_id=1, source_target_pairs={{8,0},{16,8},{24,16},{9,1},{17,9},{25,17},{10,2},{18,10},{26,18},{... | collective-permute-start | bytes 221192 | tf_op jit(solution)/shard_map/ppermute | solution.py:21
  173.3 145.2 %copy-start.16 = (bf16[1,32,32,384]{3,2,1,0:T(8,128)(2,1)S(1)}, bf16[1,32,32,384]{3,2,1,0:T(8,128)(2,1)}, u32[]{:S(2)}) copy-start(bf16[1,32,32,384]{3,2,1,0:T(8,128)(2,1)} %copy-done.15) | copy-start | bytes 2359300
  322.7 317.8 %all-reduce.9.cloned.1.call-start = ((), (), s32[]{:S(2)}) async-start(), calls=%async_computation.7 | async-start | bytes 1351680 | tf_op jit(solution)/shard_map/psum | solution.py:163
  343.1 8.8 %collective-permute-start.10 = (bf16[1,38,3,384]{3,2,1,0:T(4,128)(2,1)S(1)}, bf16[1,38,3,384]{3,2,1,0:T(4,128)(2,1)}, u32[]{:S(2)}, u32[]{:S(2)}) collective-permute-start(bf16[1,38,3,384]{3,2,1,0:T(4,128)(2,1)S(1)} %get-tuple-element.194), channel_id=1, source_target_pairs={{0,1},{1,2},{2,3},{3,4},{4,5},{5,6},{6,7},{8,9},{9,10},{10,11},{11... | collective-permute-start | bytes 262664 | tf_op jit(solution)/shard_map/ppermute | solution.py:20
  345.1 7.2 collective-permute-start.11
  408.2 314.4 %all-reduce.7.cloned.1.call-start = ((), (), s32[]{:S(2)}) async-start(), calls=%async_computation.6 | async-start | bytes 172032 | tf_op jit(solution)/shard_map/psum | solution.py:10
  (117 other events, 4114.1 us)
Sparse Core Ops, SparseCore 0:
  10.6 64.3 all-gather.3
  77.6 60.8 all-gather.5
  147.5 81.9 reduce-scatter.4
  322.8 85.3 reduce-scatter.2
  411.5 228.9 all-reduce.8
  643.0 79.6 all-reduce.6
